TPU v7x, 128 devices: a whole 4x4x4 slice. The times are simulated.
128 devices in a mesh: row: 8 (over y, core), col: 16 (over x, z).
Axes of the slice: x: 4, y: 4, z: 4, core: 2. Of those that a mesh axis runs over, the one named last changes fastest.
Arguments:
- contribution: float32 [8, 8, 4, 16, 128, 128], P(None, 'row', None, 'col'), may hold values from -6 to 6
- parent_tiles: float32 [16, 8, 8, 16, 128, 128], P(None, 'row', None, 'col'), may hold values from -6 to 6
- row_basis: float32 [8, 8, 64, 128], P(None, 'row'), may hold values from -2.4 to 2.4
- pivot_basis: float32 [8, 8, 64, 2048], P(None, 'row', None, 'col'), may hold values from -0.125 to 0.125
- tile_ranks: int32 [64], replicated, may hold values from 16 to 64, as said below
- block_map: int32 [64], replicated, may hold values from 0 to 127, as said below
- panel_start: int32 [1], replicated, may hold values from 0 to 63
- pivot_inverse: float32 [512, 512], replicated
Outputs:
- updated_parent: float32 [16, 8, 8, 16, 128, 128], P(None, 'row', None, 'col')
Inputs may be any that keep to these rules, and one draw needn't show every extreme that they name: `tile_ranks`: multiples of 16; both 16 and 64 occur. `block_map`: child tile row u * 16 + l, for 0 <= l < 16, maps to parent tile row 2 * 16 * u + h_u + l with 0 <= h_u < 16; the 4 values h_u are distinct modulo 8.
All inputs are finite; a program needn't handle non-finite values.
Results may differ from a plain program's by a relative error of at most 0.0003.
Values sent between devices are 32-bit elements; how exact they have to be, the bound alone decides.
No kernel may reach another device: no remote copies, remote signals or barrier semaphores. Data moves between devices by JAX's collectives and lax.ppermute only.
A program may use at most 128 MiB of HBM per device.

v0:
```python
import jax
import jax.numpy as jnp
from jax import lax
from jax.sharding import PartitionSpec as P

PANEL_T = 4
highest = lax.Precision.HIGHEST


def spread_2(x, axis, root):
    mine = lax.axis_index(axis) == root
    return lax.psum(jnp.where(mine, x, jnp.zeros_like(x)), axis)


def from_behind(x, axis, by):
    count = lax.axis_size(axis)
    return lax.ppermute(x, axis, [(i, (i + by) % count) for i in range(count)])


def select_entries(lookup, wanted):
    matches = wanted[:, None] == jnp.arange(lookup.shape[0], dtype=jnp.int32)[None, :]
    return jnp.sum(jnp.where(matches, lookup[None, :], 0), axis=1)


def keep_ranks(factor, tile_index, rank_table):
    limits = select_entries(rank_table, tile_index)
    kept_cols = (jnp.arange(factor.shape[1], dtype=jnp.int32)[None, :] < limits[:, None]).astype(
        jnp.float32
    )
    return factor * kept_cols[:, :, None]


def every_other(stacked, groups, offset):
    shaped = stacked.reshape((groups, stacked.shape[0] // groups) + stacked.shape[1:])
    return lax.dynamic_index_in_dim(shaped, offset, axis=1, keepdims=False)


def per_device(
    contribution,
    parent_tiles,
    row_basis,
    pivot_basis,
    tile_ranks,
    block_map,
    panel_start,
    pivot_inverse,
):
    rows_grid = lax.axis_size("row")
    cols_grid = lax.axis_size("col")
    my_row = lax.axis_index("row")
    my_col = lax.axis_index("col")
    local_rows = contribution.shape[0]
    local_cols = contribution.shape[2]
    parent_rows = parent_tiles.shape[0]
    parent_cols = parent_tiles.shape[2]
    rank_max = row_basis.shape[2]
    per_block = cols_grid // rows_grid
    row_index = jnp.arange(local_rows, dtype=jnp.int32) * rows_grid + my_row
    col_index = jnp.arange(local_cols, dtype=jnp.int32) * cols_grid + my_col
    root_row = my_col % rows_grid
    offset = my_col // rows_grid
    own_basis = keep_ranks(row_basis[:, 0], row_index, tile_ranks)
    own_pivots = pivot_basis[:, 0]
    basis_picked = every_other(row_basis[:, 0], local_cols, offset)
    col_basis = spread_2(basis_picked, "row", root_row)
    all_pivots = lax.all_gather(pivot_basis, "row", axis=1, tiled=True)
    pivot_width = pivot_basis.shape[3]
    grouped = all_pivots.reshape(local_cols, cols_grid, rank_max, pivot_width)
    products = jnp.einsum(
        "trp,scup->cstru",
        own_pivots,
        grouped,
        precision=highest,
        preferred_element_type=jnp.float32,
    )
    weights = lax.psum_scatter(
        products.reshape(lax.axis_size("col") * local_cols, local_rows, rank_max * rank_max),
        "col",
        scatter_dimension=0,
        tiled=True,
    )
    weights = weights.reshape(local_cols, local_rows, rank_max, rank_max)
    col_basis = keep_ranks(col_basis, col_index, tile_ranks)
    half_product = jnp.einsum(
        "trx,stru->tsux", own_basis, weights, precision=highest, preferred_element_type=jnp.float32
    )
    update = jnp.einsum(
        "tsux,suy->tsxy",
        half_product,
        col_basis,
        precision=highest,
        preferred_element_type=jnp.float32,
    )
    lower_mask = (row_index[:, None] >= col_index[None, :])[:, :, None, None]
    payload = jnp.where(lower_mask, contribution[:, 0, :, 0] - update, jnp.float32(0.0))
    block_first = jnp.arange(local_cols, dtype=jnp.int32) * cols_grid
    shifts = select_entries(block_map, block_first) - 2 * block_first
    row_shift = jnp.repeat(shifts, per_block) % rows_grid
    for bit_index in range((rows_grid - 1).bit_length()):
        arrived = from_behind(payload, "row", 1 << bit_index)
        taken = row_shift // (1 << bit_index) % 2 == 1
        payload = jnp.where(taken[:, None, None, None], arrived, payload)
    for bit_index in range((cols_grid - 1).bit_length()):
        arrived = from_behind(payload, "col", 1 << bit_index)
        taken = shifts // (1 << bit_index) % 2 == 1
        payload = jnp.where(taken[None, :, None, None], arrived, payload)
    row_source = (my_row - row_shift) % rows_grid
    target_rows = (
        select_entries(block_map, jnp.arange(local_rows, dtype=jnp.int32) * rows_grid + row_source)
        // rows_grid
    )
    col_source = (my_col - shifts) % cols_grid
    target_cols = (
        select_entries(block_map, jnp.arange(local_cols, dtype=jnp.int32) * cols_grid + col_source)
        // cols_grid
    )
    row_place = (jnp.arange(parent_rows, dtype=jnp.int32)[:, None] == target_rows[None, :]).astype(
        jnp.float32
    )
    col_place = (jnp.arange(parent_cols, dtype=jnp.int32)[:, None] == target_cols[None, :]).astype(
        jnp.float32
    )
    spread = jnp.einsum(
        "at,tsxy->asxy", row_place, payload, precision=highest, preferred_element_type=jnp.float32
    )
    spread = jnp.einsum(
        "bs,asxy->abxy", col_place, spread, precision=highest, preferred_element_type=jnp.float32
    )
    assembled = parent_tiles[:, 0, :, 0] + spread
    start_col = panel_start[0]
    panel_parts = []
    for panel_index in range(PANEL_T):
        column_id = start_col + panel_index
        column = lax.dynamic_index_in_dim(assembled, column_id // cols_grid, axis=1, keepdims=False)
        panel_parts.append(spread_2(column, "col", column_id % cols_grid))
    row_panel = jnp.concatenate(panel_parts, axis=2)
    col_panel = spread_2(every_other(row_panel, parent_cols, offset), "row", root_row)
    scaled = jnp.einsum(
        "axp,pq->axq",
        row_panel,
        pivot_inverse,
        precision=highest,
        preferred_element_type=jnp.float32,
    )
    trailing = jnp.einsum(
        "axq,byq->abxy", scaled, col_panel, precision=highest, preferred_element_type=jnp.float32
    )
    big_rows = jnp.arange(parent_rows, dtype=jnp.int32) * rows_grid + my_row
    big_cols = jnp.arange(parent_cols, dtype=jnp.int32) * cols_grid + my_col
    window = (big_rows[:, None] >= big_cols[None, :]) & (big_cols[None, :] >= start_col + PANEL_T)
    result = jnp.where(window[:, :, None, None], assembled - trailing, assembled)
    return result[:, None, :, None]


def solution(mesh):
    placed = (
        P(None, "row", None, "col", None, None),
        P(None, "row", None, "col", None, None),
        P(None, "row", None, None),
        P(None, "row", None, "col"),
        P(),
        P(),
        P(),
        P(),
    )
    return jax.shard_map(
        per_device,
        mesh=mesh,
        in_specs=placed,
        out_specs=P(None, "row", None, "col", None, None),
        check_vma=False,
    )
```

profile of v0, /device:TPU:0, one launch (start us, length us, event | category | flops | bytes accessed | tf_op | source)
XLA Modules:
  0.0 810.4 jit_solution(2350074608308215927)
XLA Ops:
  7.3 29.4 %all-gather.2.cloned.1.call-done = f32[8,8,64,128]{3,2,1,0:T(8,128)} async-done(((f32[8,1,64,128]{3,2,1,0:T(8,128)}), f32[8,8,64,128]{3,2,1,0:T(8,128)}) %all-gather.2.cloned.1.call-update) | async-done | bytes 2097168 | tf_op jit(solution)/shard_map/all_gather | solution.py:66
  36.7 17.0 %convolution_bitcast_fusion = f32[16,4,8,64,64]{3,4,2,0,1:T(8,128)} fusion(f32[4,16,64,128,1]{3,2,4,1,0:T(8,128)} %bitcast.109, f32[8,1,64,128]{3,2,1,0:T(8,128)} %param.11), kind=kOutput, calls=%fused_computation.1 | convolution fusion | flops 3221225472 | bytes 10747904 | tf_op jit(solution)/shard_map/trp,scup->cstru/dot_general | solution.py:69
  53.7 17.6 %copy.33 = f32[16,4,8,64,64]{4,3,2,1,0:T(8,128)} copy(f32[16,4,8,64,64]{3,4,2,0,1:T(8,128)} %convolution_bitcast_fusion) | data formatting | bytes 16777216 | tf_op jit(solution)/shard_map/trp,scup->cstru/transpose | solution.py:69
  71.3 14.7 %reshape.468 = f32[64,8,4096]{2,1,0:T(8,128)} reshape(f32[16,4,8,64,64]{4,3,2,1,0:T(8,128)} %copy.33) | data formatting | bytes 16777216 | tf_op jit(solution)/shard_map/reshape | solution.py:77
  90.2 81.4 %reduce-scatter.2.cloned.1.call-done = f32[4,8,4096]{2,1,0:T(8,128)} async-done(((f32[64,8,4096]{2,1,0:T(8,128)}), f32[4,8,4096]{2,1,0:T(8,128)}) %reduce-scatter.2.cloned.1.call-update) | async-done | bytes 524304 | tf_op jit(solution)/shard_map/reduce_scatter | solution.py:76
  176.0 56.6 %all-reduce.5.cloned.1.call-done = f32[4,64,128]{2,1,0:T(8,128)} async-done(((f32[4,64,128]{2,1,0:T(8,128)}), f32[4,64,128]{2,1,0:T(8,128)}) %all-reduce.5.cloned.1.call-update) | async-done | bytes 131088 | tf_op jit(solution)/shard_map/psum | solution.py:12
  232.6 3.9 fusion.9
  237.0 26.3 %collective-permute-done = f32[8,4,128,128]{2,3,0,1:T(8,128)} collective-permute-done((f32[8,4,128,128]{2,3,0,1:T(8,128)S(1)}, f32[8,4,128,128]{2,3,0,1:T(8,128)}, u32[]{:S(2)}, u32[]{:S(2)}) %collective-permute-start) | collective-permute-done | bytes 2097184 | tf_op jit(solution)/shard_map/ppermute | solution.py:17
  265.3 45.3 %collective-permute-done.1 = f32[8,4,128,128]{2,3,0,1:T(8,128)S(1)} collective-permute-done((f32[8,4,128,128]{2,3,0,1:T(8,128)S(1)}, f32[8,4,128,128]{2,3,0,1:T(8,128)S(1)}, u32[]{:S(2)}, u32[]{:S(2)}) %collective-permute-start.1) | collective-permute-done | bytes 2097184 | tf_op jit(solution)/shard_map/ppermute | solution.py:17
  311.9 45.3 %collective-permute-done.2 = f32[8,4,128,128]{2,3,0,1:T(8,128)S(1)} collective-permute-done((f32[8,4,128,128]{2,3,0,1:T(8,128)S(1)}, f32[8,4,128,128]{2,3,0,1:T(8,128)S(1)}, u32[]{:S(2)}, u32[]{:S(2)}) %collective-permute-start.2) | collective-permute-done | bytes 2097184 | tf_op jit(solution)/shard_map/ppermute | solution.py:17
  359.7 47.1 %collective-permute-done.3 = f32[8,4,128,128]{2,3,0,1:T(8,128)S(1)} collective-permute-done((f32[8,4,128,128]{2,3,0,1:T(8,128)S(1)}, f32[8,4,128,128]{2,3,0,1:T(8,128)S(1)}, u32[]{:S(2)}, u32[]{:S(2)}) %collective-permute-start.3) | collective-permute-done | bytes 2097184 | tf_op jit(solution)/shard_map/ppermute | solution.py:17
  407.3 49.8 %collective-permute-done.4 = f32[8,4,128,128]{2,3,0,1:T(8,128)S(1)} collective-permute-done((f32[8,4,128,128]{2,3,0,1:T(8,128)S(1)}, f32[8,4,128,128]{2,3,0,1:T(8,128)S(1)}, u32[]{:S(2)}, u32[]{:S(2)}) %collective-permute-start.4) | collective-permute-done | bytes 2097184 | tf_op jit(solution)/shard_map/ppermute | solution.py:17
  457.6 65.4 %collective-permute-done.5 = f32[8,4,128,128]{2,3,0,1:T(8,128)S(1)} collective-permute-done((f32[8,4,128,128]{2,3,0,1:T(8,128)S(1)}, f32[8,4,128,128]{2,3,0,1:T(8,128)S(1)}, u32[]{:S(2)}, u32[]{:S(2)}) %collective-permute-start.5) | collective-permute-done | bytes 2097184 | tf_op jit(solution)/shard_map/ppermute | solution.py:17
  524.5 26.5 %collective-permute-done.6 = f32[8,4,128,128]{2,3,0,1:T(8,128)} collective-permute-done((f32[8,4,128,128]{2,3,0,1:T(8,128)S(1)}, f32[8,4,128,128]{2,3,0,1:T(8,128)}, u32[]{:S(2)}, u32[]{:S(2)}) %collective-permute-start.6) | collective-permute-done | bytes 2097184 | tf_op jit(solution)/shard_map/ppermute | solution.py:17
  551.0 3.2 broadcast_select_fusion.7
  558.2 13.0 %bitcast_add_fusion = f32[16,8,128,128]{3,1,2,0:T(8,128)S(1)} fusion(f32[16,1,8,1,128,128]{5,4,3,2,1,0:T(8,128)} %param.9, f32[16,4,128,128]{3,0,2,1:T(8,128)S(1)} %fusion.21, s32[4]{0:T(128)S(1)} %and_select_fusion), kind=kOutput, calls=%fused_computation.3 | convolution fusion | flops 102760480 | bytes 20971536 | tf_op jit(solution)/shard_map/bs,asxy->abxy/dot_general | solution.py:126
  572.4 5.8 broadcast_select_fusion
  581.1 104.7 %all-reduce.9.cloned.1.call-done = (f32[16,128,128]{2,1,0:T(8,128)}, f32[16,128,128]{2,1,0:T(8,128)}, f32[16,128,128]{2,1,0:T(8,128)}, f32[16,128,128]{2,1,0:T(8,128)}) async-done(((f32[16,128,128]{2,1,0:T(8,128)}, f32[16,128,128]{2,1,0:T(8,128)}, f32[16,128,128]{2,1,0:T(8,128)}, f32[16,128,128]{2,1,0:T(8,128)}), (f32[16,128,128]{2,1,0:T(8,128)}, f32[16,128,128]{2,1,0:T(8,128)}, f32[16,128,128]{2,1,0:T(8,128)}, ...) | async-done | bytes 4194320 | tf_op jit(solution)/shard_map/psum | solution.py:12
  692.5 9.9 %fusion.10 = f32[16,128,512]{2,1,0:T(8,128)} fusion(f32[16,128,512]{2,1,0:T(8,128)} %copy-done.2, f32[512,512]{1,0:T(8,128)S(1)} %copy-done), kind=kOutput, calls=%fused_computation.14 | convolution fusion | flops 6442450944 | bytes 9437184 | tf_op jit(solution)/shard_map/axp,pq->axq/dot_general | solution.py:138
  702.4 55.5 %all-reduce.7.cloned.1.call-done = f32[8,128,512]{2,1,0:T(8,128)} async-done(((f32[8,128,512]{2,1,0:T(8,128)}), f32[8,128,512]{2,1,0:T(8,128)}) %all-reduce.7.cloned.1.call-update) | async-done | bytes 2097168 | tf_op jit(solution)/shard_map/psum | solution.py:12
  757.9 18.0 %fusion.1 = f32[8,128,16,128]{3,1,2,0:T(8,128)} fusion(f32[16,128,512]{2,1,0:T(8,128)} %fusion.10, f32[8,128,512]{2,1,0:T(8,128)} %all-reduce.7.cloned.1.call-done), kind=kOutput, calls=%fused_computation.4 | convolution fusion | flops 12884901888 | bytes 14680064 | tf_op jit(solution)/shard_map/axq,byq->abxy/dot_general | solution.py:145
  775.9 9.4 %copy.42 = f32[8,128,16,128]{1,0,3,2:T(8,128)} copy(f32[8,128,16,128]{3,1,2,0:T(8,128)} %fusion.1) | data formatting | bytes 16777216 | tf_op jit(solution)/shard_map/axq,byq->abxy/dot_general | solution.py:145
  785.3 10.2 %fusion = f32[16,1,8,1,128,128]{5,2,4,0,3,1:T(8,128)} fusion(f32[16,8,128,128]{3,1,2,0:T(8,128)} %copy-done.1, f32[8,128,16,128]{1,0,3,2:T(8,128)} %copy.42, pred[16,8]{1,0:T(8,128)(4,1)S(1)} %compare_and_fusion), kind=kLoop, calls=%fused_computation.2 | loop fusion | flops 4194304 | bytes 25165952 | tf_op jit(solution)/shard_map/broadcast_in_dim | solution.py:152
  795.4 8.2 %copy.43 = f32[16,1,8,1,128,128]{5,4,3,2,1,0:T(8,128)} copy(f32[16,1,8,1,128,128]{5,2,4,0,3,1:T(8,128)} %fusion) | data formatting | bytes 16777216 | tf_op jit(solution)/shard_map/broadcast_in_dim | solution.py:152
  (80 shorter events, 31.7 us)
Async XLA Ops:
  6.5 686.0 %copy-start = (f32[512,512]{1,0:T(8,128)S(1)}, f32[512,512]{1,0:T(8,128)}, u32[]{:S(2)}) copy-start(f32[512,512]{1,0:T(8,128)} %param.15) | copy-start | bytes 3145732
  6.5 30.2 %all-gather.2.cloned.1.call-start = ((), (), s32[]{:S(2)}) async-start(), calls=%async_computation.2 | async-start | bytes 2359296 | tf_op jit(solution)/shard_map/all_gather | solution.py:66
  7.3 164.4 %reduce-scatter.2.cloned.1.call-start = ((), (), s32[]{:S(2)}) async-start(), calls=%async_computation.3 | async-start | bytes 8912896 | tf_op jit(solution)/shard_map/reduce_scatter | solution.py:76
  86.1 0.9 copy-start.7
  86.1 1.8 copy-start.8
  86.1 2.3 copy-start.3
  86.1 146.5 %all-reduce.5.cloned.1.call-start = ((), (), s32[]{:S(2)}) async-start(), calls=%async_computation.1 | async-start | bytes 262144 | tf_op jit(solution)/shard_map/psum | solution.py:12
  87.7 598.1 %all-reduce.9.cloned.1.call-start = ((), (), s32[]{:S(2)}) async-start(), calls=%async_computation.5 | async-start | bytes 8388608 | tf_op jit(solution)/shard_map/psum | solution.py:12
  176.0 60.6 %copy-start.9 = (s32[64]{0:T(128)S(1)}, s32[64]{0:T(128)}, u32[]{:S(2)}) copy-start(s32[64]{0:T(128)} %param.13) | copy-start | bytes 772
  236.6 26.8 %collective-permute-start = (f32[8,4,128,128]{2,3,0,1:T(8,128)S(1)}, f32[8,4,128,128]{2,3,0,1:T(8,128)}, u32[]{:S(2)}, u32[]{:S(2)}) collective-permute-start(f32[8,4,128,128]{2,3,0,1:T(8,128)S(1)} %fusion.9), channel_id=1, source_target_pairs={{0,16},{16,32},{32,48},{48,64},{64,80},{80,96},{96,112},{112,0},{1... | collective-permute-start | bytes 6291464 | tf_op jit(solution)/shard_map/ppermute | solution.py:17
  265.3 45.4 %collective-permute-start.1 = (f32[8,4,128,128]{2,3,0,1:T(8,128)S(1)}, f32[8,4,128,128]{2,3,0,1:T(8,128)S(1)}, u32[]{:S(2)}, u32[]{:S(2)}) collective-permute-start(f32[8,4,128,128]{2,3,0,1:T(8,128)S(1)} %broadcast_select_fusion.1), channel_id=1, source_target_pairs={{0,32},{16,48},{32,64},{48,80},{64,96},{80,112},{96,0},{112,16},{1... | collective-permute-start | bytes 6291464 | tf_op jit(solution)/shard_map/ppermute | solution.py:17
  311.1 46.1 %collective-permute-start.2 = (f32[8,4,128,128]{2,3,0,1:T(8,128)S(1)}, f32[8,4,128,128]{2,3,0,1:T(8,128)S(1)}, u32[]{:S(2)}, u32[]{:S(2)}) collective-permute-start(f32[8,4,128,128]{2,3,0,1:T(8,128)S(1)} %broadcast_select_fusion.2), channel_id=1, source_target_pairs={{0,64},{16,80},{32,96},{48,112},{64,0},{80,16},{96,32},{112,48},{1... | collective-permute-start | bytes 6291464 | tf_op jit(solution)/shard_map/ppermute | solution.py:17
  357.6 49.2 %collective-permute-start.3 = (f32[8,4,128,128]{2,3,0,1:T(8,128)S(1)}, f32[8,4,128,128]{2,3,0,1:T(8,128)S(1)}, u32[]{:S(2)}, u32[]{:S(2)}) collective-permute-start(f32[8,4,128,128]{2,3,0,1:T(8,128)S(1)} %broadcast_select_fusion.3), channel_id=1, source_target_pairs={{0,1},{1,2},{2,3},{3,4},{4,5},{5,6},{6,7},{7,8},{8,9},{9,10},{10,1... | collective-permute-start | bytes 6291464 | tf_op jit(solution)/shard_map/ppermute | solution.py:17
  407.2 49.9 %collective-permute-start.4 = (f32[8,4,128,128]{2,3,0,1:T(8,128)S(1)}, f32[8,4,128,128]{2,3,0,1:T(8,128)S(1)}, u32[]{:S(2)}, u32[]{:S(2)}) collective-permute-start(f32[8,4,128,128]{2,3,0,1:T(8,128)S(1)} %broadcast_select_fusion.4), channel_id=1, source_target_pairs={{0,2},{1,3},{2,4},{3,5},{4,6},{5,7},{6,8},{7,9},{8,10},{9,11},{10,... | collective-permute-start | bytes 6291464 | tf_op jit(solution)/shard_map/ppermute | solution.py:17
  457.5 65.5 %collective-permute-start.5 = (f32[8,4,128,128]{2,3,0,1:T(8,128)S(1)}, f32[8,4,128,128]{2,3,0,1:T(8,128)S(1)}, u32[]{:S(2)}, u32[]{:S(2)}) collective-permute-start(f32[8,4,128,128]{2,3,0,1:T(8,128)S(1)} %broadcast_select_fusion.5), channel_id=1, source_target_pairs={{0,4},{1,5},{2,6},{3,7},{4,8},{5,9},{6,10},{7,11},{8,12},{9,13},{1... | collective-permute-start | bytes 6291464 | tf_op jit(solution)/shard_map/ppermute | solution.py:17
  523.3 27.7 %collective-permute-start.6 = (f32[8,4,128,128]{2,3,0,1:T(8,128)S(1)}, f32[8,4,128,128]{2,3,0,1:T(8,128)}, u32[]{:S(2)}, u32[]{:S(2)}) collective-permute-start(f32[8,4,128,128]{2,3,0,1:T(8,128)S(1)} %broadcast_select_fusion.6), channel_id=1, source_target_pairs={{0,8},{1,9},{2,10},{3,11},{4,12},{5,13},{6,14},{7,15},{8,0},{9,1},... | collective-permute-start | bytes 6291464 | tf_op jit(solution)/shard_map/ppermute | solution.py:17
  571.2 7.0 copy-start.1
  580.9 177.0 %all-reduce.7.cloned.1.call-start = ((), (), s32[]{:S(2)}) async-start(), calls=%async_computation.4 | async-start | bytes 4194304 | tf_op jit(solution)/shard_map/psum | solution.py:12
  685.8 1.5 copy-start.6
  685.8 1.9 copy-start.5
  687.4 1.3 copy-start.4
  688.8 2.0 copy-start.2
Sparse Core Ops, SparseCore 0:
  9.1 27.6 all-gather.1
  86.2 85.3 reduce-scatter.1
  174.0 58.6 all-reduce.4
  581.0 104.7 all-reduce.8
  692.5 65.3 all-reduce.6
where the time goes:
time: 820 us; the launch traced here: 810 us
  waiting for transfers between devices  634 us (77%)
  matrix products  66.6 us (8%)
  local copies, waits for them, and re-layouts  62.5 us (8%)
  other arithmetic  29.3 us (4%)
  between operations  14.4 us (2%)
    ppermute x7, waiting for transfers between devices, from_behind(): return lax.ppermute(x, axis, [(i, (i + by) % count) for i in range(count)])  306 us
    psum x3, waiting for transfers between devices, spread_2(): return lax.psum(jnp.where(mine, x, jnp.zeros_like(x)), axis)  217 us
    reduce_scatter x1, waiting for transfers between devices, per_device(): lax.psum_scatter(products.reshape(lax.axis_size('col') * local_cols, loca...  81.4 us
    all_gather x1, waiting for transfers between devices, per_device(): all_pivots = lax.all_gather(pivot_basis, 'row', axis=1, tiled=True)  29.4 us
    dot_general x1, matrix products, per_device(): jnp.einsum('axq,byq->abxy', scaled, col_panel, precision=highest, preferr...  18 us
    transpose x1, local copies, waits for them, and re-layouts, per_device(): jnp.einsum('trp,scup->cstru', own_pivots, grouped, precision=highest, pre...  17.6 us
    dot_general x1, matrix products, per_device(): jnp.einsum('trp,scup->cstru', own_pivots, grouped, precision=highest, pre...  17 us
  transfers between devices with their start and end apart: 12, of which 12 were waited for; matrix products, arithmetic and copies ran while one was open for 2% of the time, Pallas kernels for 0%

commit v1 on v0

--- a/solution.py
+++ b/solution.py
@@ -9,7 +9,7 @@
 
 def spread_2(x, axis, root):
     mine = lax.axis_index(axis) == root
-    return lax.psum(jnp.where(mine, x, jnp.zeros_like(x)), axis)
+    return jnp.sum(lax.all_gather(jnp.where(mine, x, jnp.zeros_like(x)), axis), axis=0)
 
 
 def from_behind(x, axis, by):

time: 820 us -> 1130 us (1.38)
  waiting for transfers between devices: 634 us -> 910 us
  other arithmetic: 29.3 us -> 70.6 us
    all_gather x0 -> x6, waiting for transfers between devices: none -> 500 us  [spread_2(): lax.all_gather(jnp.where(mine, x, jnp.zeros_like(x)), axis)]
    psum x3 -> x0, waiting for transfers between devices: 217 us -> none  [spread_2(): return lax.psum(jnp.where(mine, x, jnp.zeros_like(x)), axis)]
    reduce_sum x0 -> x6, other arithmetic: none -> 41.1 us  [spread_2(): jnp.sum(lax.all_gather(jnp.where(mine, x, jnp.zeros_like(x)), axis), axis=0)]
  transfers between devices with their start and end apart: 12 -> 15, of which waited for: 12 -> 14; matrix products, arithmetic and copies ran while one was open for 2% -> 8% of each run, Pallas kernels for 0% -> 0%
where the time goes in v1:
time: 1130 us; the launch traced here: 1120 us
  waiting for transfers between devices  910 us (81%)
  other arithmetic  70.6 us (6%)
  matrix products  64.4 us (6%)
  local copies, waits for them, and re-layouts  57 us (5%)
  between operations  15 us (1%)
    all_gather x6, waiting for transfers between devices, spread_2(): lax.all_gather(jnp.where(mine, x, jnp.zeros_like(x)), axis)  500 us
    ppermute x7, waiting for transfers between devices, from_behind(): return lax.ppermute(x, axis, [(i, (i + by) % count) for i in range(count)])  299 us
    reduce_scatter x1, waiting for transfers between devices, per_device(): lax.psum_scatter(products.reshape(lax.axis_size('col') * local_cols, loca...  80.3 us
    reduce_sum x6, other arithmetic, spread_2(): jnp.sum(lax.all_gather(jnp.where(mine, x, jnp.zeros_like(x)), axis), axis=0)  41.1 us
    all_gather x1, waiting for transfers between devices, per_device(): all_pivots = lax.all_gather(pivot_basis, 'row', axis=1, tiled=True)  27.7 us
  transfers between devices with their start and end apart: 15, of which 14 were waited for; matrix products, arithmetic and copies ran while one was open for 8% of the time, Pallas kernels for 0%

profile of v1, /device:TPU:0, one launch (start us, length us, event | category | flops | bytes accessed | tf_op | source)
XLA Modules:
  0.0 1121.2 jit_solution(16645495647349369451)
XLA Ops:
  9.0 27.7 %all-gather.14.cloned.1.call-done = f32[8,8,64,128]{3,2,1,0:T(8,128)} async-done(((f32[8,1,64,128]{3,2,1,0:T(8,128)}), f32[8,8,64,128]{3,2,1,0:T(8,128)}) %all-gather.14.cloned.1.call-update) | async-done | bytes 2097168 | tf_op jit(solution)/shard_map/all_gather | solution.py:66
  36.7 16.9 %convolution_bitcast_fusion = f32[16,4,8,64,64]{3,4,2,0,1:T(8,128)} fusion(f32[4,16,64,128,1]{3,2,4,1,0:T(8,128)} %bitcast.111, f32[8,1,64,128]{3,2,1,0:T(8,128)} %param.11), kind=kOutput, calls=%fused_computation.6 | convolution fusion | flops 3221225472 | bytes 10747904 | tf_op jit(solution)/shard_map/trp,scup->cstru/dot_general | solution.py:69
  53.7 17.7 %copy.32 = f32[16,4,8,64,64]{4,3,2,1,0:T(8,128)} copy(f32[16,4,8,64,64]{3,4,2,0,1:T(8,128)} %convolution_bitcast_fusion) | data formatting | bytes 16777216 | tf_op jit(solution)/shard_map/trp,scup->cstru/transpose | solution.py:69
  71.4 14.7 %reshape.528 = f32[64,8,4096]{2,1,0:T(8,128)} reshape(f32[16,4,8,64,64]{4,3,2,1,0:T(8,128)} %copy.32) | data formatting | bytes 16777216 | tf_op jit(solution)/shard_map/reshape | solution.py:77
  91.5 80.3 %reduce-scatter.2.cloned.1.call-done = f32[4,8,4096]{2,1,0:T(8,128)} async-done(((f32[64,8,4096]{2,1,0:T(8,128)}), f32[4,8,4096]{2,1,0:T(8,128)}) %reduce-scatter.2.cloned.1.call-update) | async-done | bytes 524304 | tf_op jit(solution)/shard_map/reduce_scatter | solution.py:76
  179.2 26.3 %collective-permute-done = f32[8,4,128,128]{2,3,0,1:T(8,128)} collective-permute-done((f32[8,4,128,128]{2,3,0,1:T(8,128)S(1)}, f32[8,4,128,128]{2,3,0,1:T(8,128)}, u32[]{:S(2)}, u32[]{:S(2)}) %collective-permute-start) | collective-permute-done | bytes 2097184 | tf_op jit(solution)/shard_map/ppermute | solution.py:17
  207.8 46.3 %collective-permute-done.1 = f32[8,4,128,128]{2,3,0,1:T(8,128)S(1)} collective-permute-done((f32[8,4,128,128]{2,3,0,1:T(8,128)S(1)}, f32[8,4,128,128]{2,3,0,1:T(8,128)S(1)}, u32[]{:S(2)}, u32[]{:S(2)}) %collective-permute-start.1) | collective-permute-done | bytes 2097184 | tf_op jit(solution)/shard_map/ppermute | solution.py:17
  256.1 44.4 %collective-permute-done.2 = f32[8,4,128,128]{2,3,0,1:T(8,128)S(1)} collective-permute-done((f32[8,4,128,128]{2,3,0,1:T(8,128)S(1)}, f32[8,4,128,128]{2,3,0,1:T(8,128)S(1)}, u32[]{:S(2)}, u32[]{:S(2)}) %collective-permute-start.2) | collective-permute-done | bytes 2097184 | tf_op jit(solution)/shard_map/ppermute | solution.py:17
  302.5 46.8 %collective-permute-done.3 = f32[8,4,128,128]{2,3,0,1:T(8,128)S(1)} collective-permute-done((f32[8,4,128,128]{2,3,0,1:T(8,128)S(1)}, f32[8,4,128,128]{2,3,0,1:T(8,128)S(1)}, u32[]{:S(2)}, u32[]{:S(2)}) %collective-permute-start.3) | collective-permute-done | bytes 2097184 | tf_op jit(solution)/shard_map/ppermute | solution.py:17
  349.8 49.8 %collective-permute-done.4 = f32[8,4,128,128]{2,3,0,1:T(8,128)S(1)} collective-permute-done((f32[8,4,128,128]{2,3,0,1:T(8,128)S(1)}, f32[8,4,128,128]{2,3,0,1:T(8,128)S(1)}, u32[]{:S(2)}, u32[]{:S(2)}) %collective-permute-start.4) | collective-permute-done | bytes 2097184 | tf_op jit(solution)/shard_map/ppermute | solution.py:17
  400.1 59.1 %collective-permute-done.5 = f32[8,4,128,128]{2,3,0,1:T(8,128)S(1)} collective-permute-done((f32[8,4,128,128]{2,3,0,1:T(8,128)S(1)}, f32[8,4,128,128]{2,3,0,1:T(8,128)S(1)}, u32[]{:S(2)}, u32[]{:S(2)}) %collective-permute-start.5) | collective-permute-done | bytes 2097184 | tf_op jit(solution)/shard_map/ppermute | solution.py:17
  460.8 26.5 %collective-permute-done.6 = f32[8,4,128,128]{2,3,0,1:T(8,128)} collective-permute-done((f32[8,4,128,128]{2,3,0,1:T(8,128)S(1)}, f32[8,4,128,128]{2,3,0,1:T(8,128)}, u32[]{:S(2)}, u32[]{:S(2)}) %collective-permute-start.6) | collective-permute-done | bytes 2097184 | tf_op jit(solution)/shard_map/ppermute | solution.py:17
  494.4 13.0 %bitcast_add_fusion = f32[16,8,128,128]{3,1,2,0:T(8,128)S(1)} fusion(f32[16,1,8,1,128,128]{5,4,3,2,1,0:T(8,128)} %param.9, f32[16,4,128,128]{3,0,2,1:T(8,128)S(1)} %fusion.19, s32[4]{0:T(128)S(1)} %and_select_fusion), kind=kOutput, calls=%fused_computation.8 | convolution fusion | flops 102760480 | bytes 20971536 | tf_op jit(solution)/shard_map/bs,asxy->abxy/dot_general | solution.py:126
  515.5 109.0 %all-gather.24.cloned.1.call-done = f32[256,1,128,128]{3,2,1,0:T(8,128)} async-done(((f32[16,1,128,128]{3,2,1,0:T(8,128)}), f32[256,1,128,128]{3,2,1,0:T(8,128)}) %all-gather.24.cloned.1.call-update) | async-done | bytes 16777232 | tf_op jit(solution)/shard_map/all_gather | solution.py:12
  632.0 105.6 %all-gather.22.cloned.1.call-done = f32[256,1,128,128]{3,2,1,0:T(8,128)} async-done(((f32[16,1,128,128]{3,2,1,0:T(8,128)}), f32[256,1,128,128]{3,2,1,0:T(8,128)}) %all-gather.22.cloned.1.call-update) | async-done | bytes 16777232 | tf_op jit(solution)/shard_map/all_gather | solution.py:12
  745.1 105.6 %all-gather.20.cloned.1.call-done = f32[256,1,128,128]{3,2,1,0:T(8,128)} async-done(((f32[16,1,128,128]{3,2,1,0:T(8,128)}), f32[256,1,128,128]{3,2,1,0:T(8,128)}) %all-gather.20.cloned.1.call-update) | async-done | bytes 16777232 | tf_op jit(solution)/shard_map/all_gather | solution.py:12
  850.7 8.4 bitcast_reduce_fusion.3
  859.1 104.8 %all-gather.18.cloned.1.call-done = f32[256,1,128,128]{3,2,1,0:T(8,128)} async-done(((f32[16,1,128,128]{3,2,1,0:T(8,128)}), f32[256,1,128,128]{3,2,1,0:T(8,128)}) %all-gather.18.cloned.1.call-update) | async-done | bytes 16777232 | tf_op jit(solution)/shard_map/all_gather | solution.py:12
  963.9 8.4 bitcast_reduce_fusion.4
  976.0 9.5 fusion.9
  985.5 75.1 %all-gather.26.cloned.1.call-done = f32[64,1,128,512]{3,2,1,0:T(8,128)} async-done(((f32[8,1,128,512]{3,2,1,0:T(8,128)}), f32[64,1,128,512]{3,2,1,0:T(8,128)}) %all-gather.26.cloned.1.call-update) | async-done | bytes 16777232 | tf_op jit(solution)/shard_map/all_gather | solution.py:12
  1068.7 17.6 %fusion.1 = f32[8,128,16,128]{3,1,2,0:T(8,128)} fusion(f32[16,128,512]{2,1,0:T(8,128)} %fusion.9, f32[8,128,512]{2,1,0:T(8,128)S(1)} %bitcast_reduce_fusion), kind=kOutput, calls=%fused_computation.10 | convolution fusion | flops 12884901888 | bytes 14680064 | tf_op jit(solution)/shard_map/axq,byq->abxy/dot_general | solution.py:145
  1086.3 9.3 copy.40
  1095.5 10.1 fusion
  (81 shorter events, 73.0 us)
Async XLA Ops:
  6.5 969.5 %copy-start = (f32[512,512]{1,0:T(8,128)S(1)}, f32[512,512]{1,0:T(8,128)}, u32[]{:S(2)}) copy-start(f32[512,512]{1,0:T(8,128)} %param.15) | copy-start | bytes 3145732
  6.5 30.2 %all-gather.14.cloned.1.call-start = ((), (), s32[]{:S(2)}) async-start(), calls=%async_computation.1 | async-start | bytes 2359296 | tf_op jit(solution)/shard_map/all_gather | solution.py:66
  7.3 82.9 %all-gather.16.cloned.1.call-start = ((), (), s32[]{:S(2)}) async-start(), calls=%async_computation.3 | async-start | bytes 1179648 | tf_op jit(solution)/shard_map/all_gather | solution.py:12
  8.9 162.9 %reduce-scatter.2.cloned.1.call-start = ((), (), s32[]{:S(2)}) async-start(), calls=%async_computation.2 | async-start | bytes 8912896 | tf_op jit(solution)/shard_map/reduce_scatter | solution.py:76
  86.1 1.6 copy-start.2
  86.1 3.5 copy-start.4
  86.1 538.4 %all-gather.24.cloned.1.call-start = ((), (), s32[]{:S(2)}) async-start(), calls=%async_computation.7 | async-start | bytes 17825792 | tf_op jit(solution)/shard_map/all_gather | solution.py:12
  89.6 83.7 %copy-start.3 = (f32[8,1,64,128]{3,2,1,0:T(8,128)S(1)}, f32[8,1,64,128]{3,2,1,0:T(8,128)}, u32[]{:S(2)}) copy-start(f32[8,1,64,128]{3,2,1,0:T(8,128)} %param.10) | copy-start | bytes 786436
  175.2 3.6 copy-start.5
  178.8 26.8 %collective-permute-start = (f32[8,4,128,128]{2,3,0,1:T(8,128)S(1)}, f32[8,4,128,128]{2,3,0,1:T(8,128)}, u32[]{:S(2)}, u32[]{:S(2)}) collective-permute-start(f32[8,4,128,128]{2,3,0,1:T(8,128)S(1)} %fusion.8), channel_id=1, source_target_pairs={{0,16},{16,32},{32,48},{48,64},{64,80},{80,96},{96,112},{112,0},{1... | collective-permute-start | bytes 6291464 | tf_op jit(solution)/shard_map/ppermute | solution.py:17
  207.5 46.6 %collective-permute-start.1 = (f32[8,4,128,128]{2,3,0,1:T(8,128)S(1)}, f32[8,4,128,128]{2,3,0,1:T(8,128)S(1)}, u32[]{:S(2)}, u32[]{:S(2)}) collective-permute-start(f32[8,4,128,128]{2,3,0,1:T(8,128)S(1)} %broadcast_select_fusion.4), channel_id=1, source_target_pairs={{0,32},{16,48},{32,64},{48,80},{64,96},{80,112},{96,0},{112,16},{1... | collective-permute-start | bytes 6291464 | tf_op jit(solution)/shard_map/ppermute | solution.py:17
  254.5 46.0 %collective-permute-start.2 = (f32[8,4,128,128]{2,3,0,1:T(8,128)S(1)}, f32[8,4,128,128]{2,3,0,1:T(8,128)S(1)}, u32[]{:S(2)}, u32[]{:S(2)}) collective-permute-start(f32[8,4,128,128]{2,3,0,1:T(8,128)S(1)} %broadcast_select_fusion.5), channel_id=1, source_target_pairs={{0,64},{16,80},{32,96},{48,112},{64,0},{80,16},{96,32},{112,48},{1... | collective-permute-start | bytes 6291464 | tf_op jit(solution)/shard_map/ppermute | solution.py:17
  300.9 48.4 %collective-permute-start.3 = (f32[8,4,128,128]{2,3,0,1:T(8,128)S(1)}, f32[8,4,128,128]{2,3,0,1:T(8,128)S(1)}, u32[]{:S(2)}, u32[]{:S(2)}) collective-permute-start(f32[8,4,128,128]{2,3,0,1:T(8,128)S(1)} %broadcast_select_fusion.6), channel_id=1, source_target_pairs={{0,1},{1,2},{2,3},{3,4},{4,5},{5,6},{6,7},{7,8},{8,9},{9,10},{10,1... | collective-permute-start | bytes 6291464 | tf_op jit(solution)/shard_map/ppermute | solution.py:17
  349.7 49.9 %collective-permute-start.4 = (f32[8,4,128,128]{2,3,0,1:T(8,128)S(1)}, f32[8,4,128,128]{2,3,0,1:T(8,128)S(1)}, u32[]{:S(2)}, u32[]{:S(2)}) collective-permute-start(f32[8,4,128,128]{2,3,0,1:T(8,128)S(1)} %broadcast_select_fusion.7), channel_id=1, source_target_pairs={{0,2},{1,3},{2,4},{3,5},{4,6},{5,7},{6,8},{7,9},{8,10},{9,11},{10,... | collective-permute-start | bytes 6291464 | tf_op jit(solution)/shard_map/ppermute | solution.py:17
  400.0 59.2 %collective-permute-start.5 = (f32[8,4,128,128]{2,3,0,1:T(8,128)S(1)}, f32[8,4,128,128]{2,3,0,1:T(8,128)S(1)}, u32[]{:S(2)}, u32[]{:S(2)}) collective-permute-start(f32[8,4,128,128]{2,3,0,1:T(8,128)S(1)} %broadcast_select_fusion.8), channel_id=1, source_target_pairs={{0,4},{1,5},{2,6},{3,7},{4,8},{5,9},{6,10},{7,11},{8,12},{9,13},{1... | collective-permute-start | bytes 6291464 | tf_op jit(solution)/shard_map/ppermute | solution.py:17
  459.5 27.7 %collective-permute-start.6 = (f32[8,4,128,128]{2,3,0,1:T(8,128)S(1)}, f32[8,4,128,128]{2,3,0,1:T(8,128)}, u32[]{:S(2)}, u32[]{:S(2)}) collective-permute-start(f32[8,4,128,128]{2,3,0,1:T(8,128)S(1)} %broadcast_select_fusion.9), channel_id=1, source_target_pairs={{0,8},{1,9},{2,10},{3,11},{4,12},{5,13},{6,14},{7,15},{8,0},{9,1},... | collective-permute-start | bytes 6291464 | tf_op jit(solution)/shard_map/ppermute | solution.py:17
  507.4 5.9 copy-start.1
  513.4 224.3 %all-gather.22.cloned.1.call-start = ((), (), s32[]{:S(2)}) async-start(), calls=%async_computation.6 | async-start | bytes 17825792 | tf_op jit(solution)/shard_map/all_gather | solution.py:12
  514.0 336.7 %all-gather.20.cloned.1.call-start = ((), (), s32[]{:S(2)}) async-start(), calls=%async_computation.5 | async-start | bytes 17825792 | tf_op jit(solution)/shard_map/all_gather | solution.py:12
  514.5 449.4 %all-gather.18.cloned.1.call-start = ((), (), s32[]{:S(2)}) async-start(), calls=%async_computation.4 | async-start | bytes 17825792 | tf_op jit(solution)/shard_map/all_gather | solution.py:12
  515.3 545.3 %all-gather.26.cloned.1.call-start = ((), (), s32[]{:S(2)}) async-start(), calls=%async_computation.8 | async-start | bytes 18874368 | tf_op jit(solution)/shard_map/all_gather | solution.py:12
Sparse Core Ops, SparseCore 0:
  9.1 27.6 all-gather.13
  38.4 23.6 all-gather.15
  86.2 85.5 reduce-scatter.1
  513.5 111.0 all-gather.23
  626.5 111.0 all-gather.21
  739.6 111.0 all-gather.19
  852.8 111.0 all-gather.17
  976.0 84.5 all-gather.25
